TPU v7x, 256 devices: a whole 4x4x8 slice. The times are simulated.
256 devices in a mesh: row: 8 (over x, core), col: 32 (over y, z).
Axes of the slice: x: 4, y: 4, z: 8, core: 2. Of those that a mesh axis runs over, the one named last changes fastest.
Arguments:
- matrix: float32 [16384, 16384], P('row', 'col'), as said below
- panel: float32 [16384, 256], P(('row', 'col')), may hold values from -0.046875 to 0.046875
- factor: float32 [256, 256], replicated, as said below
Outputs:
- updated: float32 [16384, 16384], P('row', 'col')
- correction: float32 [16384, 256], P(('row', 'col'))
Inputs may be any that keep to these rules, and one draw needn't show every extreme that they name: `matrix`: symmetric. `factor`: upper triangular with a positive diagonal.
All inputs are finite; a program needn't handle non-finite values.
Results may differ from a plain program's by a relative error of at most 0.000071.
Values sent between devices are 32-bit elements; how exact they have to be, the bound alone decides.
No kernel may reach another device: no remote copies, remote signals or barrier semaphores. Data moves between devices by JAX's collectives and lax.ppermute only.
A program may use at most 64 MiB of HBM per device.

v0:
```python
import jax
import jax.numpy as jnp
from jax import lax
from jax.sharding import PartitionSpec as P


def from_root(value, axis, source):
    kept = jnp.where(lax.axis_index(axis) == source, value, 0).astype(value.dtype)
    return lax.psum(kept, axis)


def mult(left, right):
    return jnp.dot(left, right, precision=lax.Precision.HIGHEST, preferred_element_type=jnp.float32)


def per_device(matrix, panel, factor):
    ncols = lax.axis_size("col")
    nrows = lax.axis_size("row")
    blocks = panel.shape[0]
    col_index = lax.axis_index("col")
    col_rows = blocks * nrows
    offset = col_index * nrows % ncols * blocks
    owner = col_index * nrows // ncols
    row_panel = lax.all_gather(panel, "col", axis=0, tiled=True)
    col_panel = from_root(lax.dynamic_slice_in_dim(row_panel, offset, col_rows, 0), "row", owner)
    product = lax.psum_scatter(mult(matrix, col_panel), "col", scatter_dimension=0, tiled=True)
    scaled = mult(product, factor)
    small = lax.psum(mult(panel.T, scaled), ("row", "col"))
    correction = scaled - 0.5 * mult(panel, mult(factor.T, small))
    row_corr = lax.all_gather(correction, "col", axis=0, tiled=True)
    col_corr = from_root(lax.dynamic_slice_in_dim(row_corr, offset, col_rows, 0), "row", owner)
    updated = matrix - mult(row_panel, col_corr.T) - mult(row_corr, col_panel.T)
    return (updated, correction)


def solution(mesh):
    in_specs = (P("row", "col"), P(("row", "col"), None), P())
    out_specs = (P("row", "col"), P(("row", "col"), None))
    return jax.shard_map(
        per_device, mesh=mesh, in_specs=in_specs, out_specs=out_specs, check_vma=False
    )
```

profile of v0, /device:TPU:8, one launch (start us, length us, event | category | flops | bytes accessed | tf_op | source)
XLA Modules:
  0.0 802.7 jit_solution(14840826598810947577)
XLA Ops:
  7.2 0.0 copy-start
  7.2 0.0 all-gather.3.cloned.1.call-start
  7.2 0.7 all-gather.3.cloned.1.call-update
  7.9 0.0 all-reduce.4.cloned.1.call-start
  8.0 82.3 %all-gather.3.cloned.1.call-done = f32[2048,256]{1,0:T(8,128)} async-done(((f32[64,256]{1,0:T(8,128)}), f32[2048,256]{1,0:T(8,128)}) %all-gather.3.cloned.1.call-update) | async-done | bytes 2097168 | tf_op jit(solution)/shard_map/all_gather | solution.py:24
  90.3 1.9 dynamic-slice_select_fusion.1
  92.1 0.0 all-reduce.4.cloned.1.call-update
  92.2 0.0 reduce-scatter.4.cloned.1.call-start
  92.2 65.1 %all-reduce.4.cloned.1.call-done = f32[512,256]{1,0:T(8,128)} async-done(((f32[512,256]{1,0:T(8,128)}), f32[512,256]{1,0:T(8,128)}) %all-reduce.4.cloned.1.call-update) | async-done | bytes 524304 | tf_op jit(solution)/shard_map/psum | solution.py:9
  157.3 8.7 %convolution_bitcast_fusion = f32[2048,256]{0,1:T(8,128)S(1)} fusion(f32[512,256]{1,0:T(8,128)} %all-reduce.4.cloned.1.call-done, f32[2048,512]{1,0:T(8,128)} %param.3), kind=kOutput, calls=%fused_computation.2 | convolution fusion | flops 3221225472 | bytes 6815744 | tf_op jit(solution)/shard_map/dot_general | solution.py:13
  166.0 0.0 copy-start.3
  166.0 1.8 copy.12
  167.8 0.0 reduce-scatter.4.cloned.1.call-update
  167.8 0.0 all-reduce.6.cloned.1.call-start
  167.9 214.8 %reduce-scatter.4.cloned.1.call-done = f32[64,256]{1,0:T(8,128)} async-done(((f32[2048,256]{1,0:T(8,128)}), f32[64,256]{1,0:T(8,128)}) %reduce-scatter.4.cloned.1.call-update) | async-done | bytes 65552
  382.7 0.0 copy-done
  382.7 1.1 fusion.3
  383.8 0.0 copy-done.3
  383.8 1.1 convolution_bitcast_fusion.1
  384.9 0.0 all-reduce.6.cloned.1.call-update
  384.9 0.0 all-gather.5.cloned.1.call-start
  385.0 252.9 %all-reduce.6.cloned.1.call-done = f32[256,256]{0,1:T(8,128)} async-done(((f32[256,256]{0,1:T(8,128)}), f32[256,256]{0,1:T(8,128)}) %all-reduce.6.cloned.1.call-update) | async-done | bytes 262160 | tf_op jit(solution)/shard_map/psum | solution.py:28
  637.9 1.3 fusion.4
  639.2 1.0 fusion.2
  640.3 0.0 all-gather.5.cloned.1.call-update
  640.3 0.0 copy-start.2
  640.3 0.0 all-reduce.8.cloned.1.call-start
  640.3 5.4 copy.8
  645.8 0.0 copy-start.1
  645.8 70.7 %all-gather.5.cloned.1.call-done = f32[2048,256]{1,0:T(8,128)} async-done(((f32[64,256]{1,0:T(8,128)}), f32[2048,256]{1,0:T(8,128)}) %all-gather.5.cloned.1.call-update) | async-done | bytes 2097168 | tf_op jit(solution)/shard_map/all_gather | solution.py:30
  716.5 1.9 dynamic-slice_select_fusion
  718.4 0.0 all-reduce.8.cloned.1.call-update
  718.4 0.0 copy-done.2
  718.4 6.9 fusion.5
  725.3 57.5 %all-reduce.8.cloned.1.call-done = f32[512,256]{1,0:T(8,128)} async-done(((f32[512,256]{1,0:T(8,128)}), f32[512,256]{1,0:T(8,128)}) %all-reduce.8.cloned.1.call-update) | async-done | bytes 524304 | tf_op jit(solution)/shard_map/psum | solution.py:9
  782.8 0.0 copy-done.1
  782.8 7.7 fusion
  790.5 5.3 copy.10
Async XLA Ops:
  7.2 375.5 %copy-start = (f32[256,256]{1,0:T(8,128)S(1)}, f32[256,256]{1,0:T(8,128)}, u32[]{:S(2)}) copy-start(f32[256,256]{1,0:T(8,128)} %param.5) | copy-start | bytes 786436
  7.2 83.1 %all-gather.3.cloned.1.call-start = ((), (), s32[]{:S(2)}) async-start(), calls=%async_computation.1 | async-start | bytes 2162688 | tf_op jit(solution)/shard_map/all_gather | solution.py:24
  7.9 149.4 %all-reduce.4.cloned.1.call-start = ((), (), s32[]{:S(2)}) async-start(), calls=%async_computation.2 | async-start | bytes 1048576 | tf_op jit(solution)/shard_map/psum | solution.py:9
  92.2 290.5 %reduce-scatter.4.cloned.1.call-start = ((), (), s32[]{:S(2)}) async-start(), calls=%async_computation.6 | async-start | bytes 2162688
  166.0 217.8 %copy-start.3 = (f32[64,256]{1,0:T(8,128)S(1)}, f32[64,256]{1,0:T(8,128)}, u32[]{:S(2)}) copy-start(f32[64,256]{1,0:T(8,128)} %param.4) | copy-start | bytes 196612
  167.8 470.1 %all-reduce.6.cloned.1.call-start = ((), (), s32[]{:S(2)}) async-start(), calls=%async_computation.3 | async-start | bytes 524288 | tf_op jit(solution)/shard_map/psum | solution.py:28
  384.9 331.5 %all-gather.5.cloned.1.call-start = ((), (), s32[]{:S(2)}) async-start(), calls=%async_computation.4 | async-start | bytes 2162688 | tf_op jit(solution)/shard_map/all_gather | solution.py:30
  640.3 78.1 %copy-start.2 = (f32[512,256]{1,0:T(8,128)S(1)}, f32[512,256]{1,0:T(8,128)}, u32[]{:S(2)}) copy-start(f32[512,256]{1,0:T(8,128)} %all-reduce.4.cloned.1.call-done) | copy-start | bytes 1572868
  640.3 142.5 %all-reduce.8.cloned.1.call-start = ((), (), s32[]{:S(2)}) async-start(), calls=%async_computation.5 | async-start | bytes 1048576 | tf_op jit(solution)/shard_map/psum | solution.py:9
  645.8 137.0 %copy-start.1 = (f32[2048,256]{1,0:T(8,128)S(1)}, f32[2048,256]{1,0:T(8,128)}, u32[]{:S(2)}) copy-start(f32[2048,256]{1,0:T(8,128)} %all-gather.3.cloned.1.call-done) | copy-start | bytes 6291460
Sparse Core Ops, SparseCore 0:
  10.6 79.6 all-gather.2
  93.2 64.0 all-reduce.3
  168.0 214.6 reduce-scatter.3
  388.6 249.2 all-reduce.5
  640.9 75.5 all-gather.4
  718.7 64.0 all-reduce.7
where the time goes:
time: 803 us
  waiting for transfers between devices  744 us (93%)
  matrix products  27.9 us (3%)
  between operations  14.2 us (2%)
  local copies, waits for them, and re-layouts  12.6 us (2%)
    psum x1, waiting for transfers between devices, per_device(): small = lax.psum(mult(panel.T, scaled), ('row', 'col'))  253 us
    unnamed x7, waiting for transfers between devices  216 us
    psum x2, waiting for transfers between devices, from_root(): return lax.psum(kept, axis)  123 us
    all_gather x1, waiting for transfers between devices, per_device(): row_panel = lax.all_gather(panel, 'col', axis=0, tiled=True)  82.3 us
    all_gather x1, waiting for transfers between devices, per_device(): row_corr = lax.all_gather(correction, 'col', axis=0, tiled=True)  70.7 us
    dot_general x7, matrix products, mult(): jnp.dot(left, right, precision=lax.Precision.HIGHEST, preferred_element_t...  27.9 us
  transfers between devices with their start and end apart: 6, of which 6 were waited for; matrix products, arithmetic and copies ran while one was open for 2% of the time, Pallas kernels for 0%

commit v1 on v0

--- a/solution.py
+++ b/solution.py
@@ -25,7 +25,7 @@
     col_panel = from_root(lax.dynamic_slice_in_dim(row_panel, offset, col_rows, 0), "row", owner)
     product = lax.psum_scatter(mult(matrix, col_panel), "col", scatter_dimension=0, tiled=True)
     scaled = mult(product, factor)
-    small = lax.psum(mult(panel.T, scaled), ("row", "col"))
+    small = lax.psum(lax.psum(mult(panel.T, scaled), "col"), "row")
     correction = scaled - 0.5 * mult(panel, mult(factor.T, small))
     row_corr = lax.all_gather(correction, "col", axis=0, tiled=True)
     col_corr = from_root(lax.dynamic_slice_in_dim(row_corr, offset, col_rows, 0), "row", owner)

time: 803 us -> 760 us (0.946)
  waiting for transfers between devices: 744 us -> 701 us
    psum x1 -> x2, waiting for transfers between devices: 253 us -> 209 us  [per_device(): small = lax.psum(lax.psum(mult(panel.T, scaled), 'col'), 'row')]
    unnamed x7 -> x8, waiting for transfers between devices: 216 us -> 216 us
  transfers between devices with their start and end apart: 6 -> 7, of which waited for: 6 -> 7; matrix products, arithmetic and copies ran while one was open for 2% -> 2% of each run, Pallas kernels for 0% -> 0%
where the time goes in v1:
time: 760 us
  waiting for transfers between devices  701 us (92%)
  matrix products  27.9 us (4%)
  between operations  14.2 us (2%)
  local copies, waits for them, and re-layouts  12.6 us (2%)
    unnamed x8, waiting for transfers between devices  216 us
    psum x2, waiting for transfers between devices, per_device(): small = lax.psum(lax.psum(mult(panel.T, scaled), 'col'), 'row')  209 us
    psum x2, waiting for transfers between devices, from_root(): return lax.psum(kept, axis)  123 us
    all_gather x1, waiting for transfers between devices, per_device(): row_panel = lax.all_gather(panel, 'col', axis=0, tiled=True)  82.3 us
    all_gather x1, waiting for transfers between devices, per_device(): row_corr = lax.all_gather(correction, 'col', axis=0, tiled=True)  71.4 us
    dot_general x7, matrix products, mult(): jnp.dot(left, right, precision=lax.Precision.HIGHEST, preferred_element_t...  27.9 us
  transfers between devices with their start and end apart: 7, of which 7 were waited for; matrix products, arithmetic and copies ran while one was open for 2% of the time, Pallas kernels for 0%

profile of v1, /device:TPU:8, one launch (start us, length us, event | category | flops | bytes accessed | tf_op | source)
XLA Modules:
  0.0 759.8 jit_solution(3837706875985428337)
XLA Ops:
  7.2 0.0 copy-start
  7.2 0.0 all-gather.3.cloned.1.call-start
  7.2 0.7 all-gather.3.cloned.1.call-update
  7.9 0.0 all-reduce.5.cloned.1.call-start
  8.0 82.3 %all-gather.3.cloned.1.call-done = f32[2048,256]{1,0:T(8,128)} async-done(((f32[64,256]{1,0:T(8,128)}), f32[2048,256]{1,0:T(8,128)}) %all-gather.3.cloned.1.call-update) | async-done | bytes 2097168 | tf_op jit(solution)/shard_map/all_gather | solution.py:24
  90.3 1.9 dynamic-slice_select_fusion.1
  92.1 0.0 all-reduce.5.cloned.1.call-update
  92.2 0.0 reduce-scatter.4.cloned.1.call-start
  92.2 65.1 %all-reduce.5.cloned.1.call-done = f32[512,256]{1,0:T(8,128)} async-done(((f32[512,256]{1,0:T(8,128)}), f32[512,256]{1,0:T(8,128)}) %all-reduce.5.cloned.1.call-update) | async-done | bytes 524304 | tf_op jit(solution)/shard_map/psum | solution.py:9
  157.3 8.7 %convolution_bitcast_fusion = f32[2048,256]{0,1:T(8,128)S(1)} fusion(f32[512,256]{1,0:T(8,128)} %all-reduce.5.cloned.1.call-done, f32[2048,512]{1,0:T(8,128)} %param.3), kind=kOutput, calls=%fused_computation.2 | convolution fusion | flops 3221225472 | bytes 6815744 | tf_op jit(solution)/shard_map/dot_general | solution.py:13
  166.0 0.0 copy-start.3
  166.0 1.8 copy.12
  167.8 0.0 reduce-scatter.4.cloned.1.call-update
  167.8 0.0 all-reduce.7.cloned.1.call-start
  167.9 214.8 %reduce-scatter.4.cloned.1.call-done = f32[64,256]{1,0:T(8,128)} async-done(((f32[2048,256]{1,0:T(8,128)}), f32[64,256]{1,0:T(8,128)}) %reduce-scatter.4.cloned.1.call-update) | async-done | bytes 65552
  382.7 0.0 copy-done
  382.7 1.1 fusion.3
  383.8 0.0 copy-done.3
  383.8 1.1 convolution_bitcast_fusion.1
  384.9 0.0 all-reduce.7.cloned.1.call-update
  384.9 0.0 all-reduce.9.cloned.1.call-start
  385.0 143.8 %all-reduce.7.cloned.1.call-done = f32[256,256]{0,1:T(8,128)} async-done(((f32[256,256]{0,1:T(8,128)}), f32[256,256]{0,1:T(8,128)}) %all-reduce.7.cloned.1.call-update) | async-done | bytes 262160 | tf_op jit(solution)/shard_map/psum | solution.py:28
  528.8 0.0 all-reduce.9.cloned.1.call-update
  528.9 0.0 all-gather.5.cloned.1.call-start
  528.9 65.1 %all-reduce.9.cloned.1.call-done = f32[256,256]{0,1:T(8,128)} async-done(((f32[256,256]{0,1:T(8,128)}), f32[256,256]{0,1:T(8,128)}) %all-reduce.9.cloned.1.call-update) | async-done | bytes 262160 | tf_op jit(solution)/shard_map/psum | solution.py:28
  594.0 1.3 fusion.4
  595.4 1.0 fusion.2
  596.4 0.0 all-gather.5.cloned.1.call-update
  596.4 0.0 copy-start.2
  596.4 0.0 all-reduce.11.cloned.1.call-start
  596.5 5.4 copy.8
  601.9 0.0 copy-start.1
  601.9 71.4 %all-gather.5.cloned.1.call-done = f32[2048,256]{1,0:T(8,128)} async-done(((f32[64,256]{1,0:T(8,128)}), f32[2048,256]{1,0:T(8,128)}) %all-gather.5.cloned.1.call-update) | async-done | bytes 2097168 | tf_op jit(solution)/shard_map/all_gather | solution.py:30
  673.3 1.9 dynamic-slice_select_fusion
  675.2 0.0 all-reduce.11.cloned.1.call-update
  675.2 0.0 copy-done.2
  675.2 6.9 fusion.5
  682.2 57.7 %all-reduce.11.cloned.1.call-done = f32[512,256]{1,0:T(8,128)} async-done(((f32[512,256]{1,0:T(8,128)}), f32[512,256]{1,0:T(8,128)}) %all-reduce.11.cloned.1.call-update) | async-done | bytes 524304 | tf_op jit(solution)/shard_map/psum | solution.py:9
  739.9 0.0 copy-done.1
  739.9 7.7 %fusion = f32[2048,512]{0,1:T(8,128)} fusion(f32[2048,512]{0,1:T(8,128)} %fusion.5, f32[2048,512]{0,1:T(8,128)} %copy.8, f32[512,256]{1,0:T(8,128)} %all-reduce.11.cloned.1.call-done, f32[2048,256]{1,0:T(8,128)S(1)} %copy-done.1), kind=kOutput, calls=%fused_computation.1 | convolution fusion | flops 3223322624 | bytes 15204352 | tf_op jit(solution)/shard_map/dot_general | solution.py:13
  747.6 5.3 copy.10
Async XLA Ops:
  7.2 375.5 %copy-start = (f32[256,256]{1,0:T(8,128)S(1)}, f32[256,256]{1,0:T(8,128)}, u32[]{:S(2)}) copy-start(f32[256,256]{1,0:T(8,128)} %param.5) | copy-start | bytes 786436
  7.2 83.1 %all-gather.3.cloned.1.call-start = ((), (), s32[]{:S(2)}) async-start(), calls=%async_computation.1 | async-start | bytes 2162688 | tf_op jit(solution)/shard_map/all_gather | solution.py:24
  7.9 149.4 %all-reduce.5.cloned.1.call-start = ((), (), s32[]{:S(2)}) async-start(), calls=%async_computation.2 | async-start | bytes 1048576 | tf_op jit(solution)/shard_map/psum | solution.py:9
  92.2 290.5 %reduce-scatter.4.cloned.1.call-start = ((), (), s32[]{:S(2)}) async-start(), calls=%async_computation.7 | async-start | bytes 2162688
  166.0 217.8 %copy-start.3 = (f32[64,256]{1,0:T(8,128)S(1)}, f32[64,256]{1,0:T(8,128)}, u32[]{:S(2)}) copy-start(f32[64,256]{1,0:T(8,128)} %param.4) | copy-start | bytes 196612
  167.8 361.0 %all-reduce.7.cloned.1.call-start = ((), (), s32[]{:S(2)}) async-start(), calls=%async_computation.3 | async-start | bytes 524288 | tf_op jit(solution)/shard_map/psum | solution.py:28
  384.9 209.1 %all-reduce.9.cloned.1.call-start = ((), (), s32[]{:S(2)}) async-start(), calls=%async_computation.4 | async-start | bytes 524288 | tf_op jit(solution)/shard_map/psum | solution.py:28
  528.9 144.5 %all-gather.5.cloned.1.call-start = ((), (), s32[]{:S(2)}) async-start(), calls=%async_computation.5 | async-start | bytes 2162688 | tf_op jit(solution)/shard_map/all_gather | solution.py:30
  596.4 78.8 %copy-start.2 = (f32[512,256]{1,0:T(8,128)S(1)}, f32[512,256]{1,0:T(8,128)}, u32[]{:S(2)}) copy-start(f32[512,256]{1,0:T(8,128)} %all-reduce.5.cloned.1.call-done) | copy-start | bytes 1572868
  596.4 143.5 %all-reduce.11.cloned.1.call-start = ((), (), s32[]{:S(2)}) async-start(), calls=%async_computation.6 | async-start | bytes 1048576 | tf_op jit(solution)/shard_map/psum | solution.py:9
  601.9 138.0 %copy-start.1 = (f32[2048,256]{1,0:T(8,128)S(1)}, f32[2048,256]{1,0:T(8,128)}, u32[]{:S(2)}) copy-start(f32[2048,256]{1,0:T(8,128)} %all-gather.3.cloned.1.call-done) | copy-start | bytes 6291460
Sparse Core Ops, SparseCore 0:
  10.6 79.6 all-gather.2
  93.2 64.0 all-reduce.4
  168.0 214.6 reduce-scatter.3
  386.6 142.2 all-reduce.6
  531.0 62.9 all-reduce.8
  597.4 75.8 all-gather.4
  675.8 64.0 all-reduce.10

commit v2 on v0

--- a/solution.py
+++ b/solution.py
@@ -6,7 +6,7 @@
 
 def from_root(value, axis, source):
     kept = jnp.where(lax.axis_index(axis) == source, value, 0).astype(value.dtype)
-    return lax.psum(kept, axis)
+    return jnp.sum(lax.all_gather(kept, axis), axis=0)
 
 
 def mult(left, right):

time: 803 us -> 749 us (0.933)
  waiting for transfers between devices: 744 us -> 685 us
    psum x2 -> x0, waiting for transfers between devices: 123 us -> none  [from_root(): return lax.psum(kept, axis)]
    all_gather x0 -> x2, waiting for transfers between devices: none -> 56.1 us  [from_root(): return jnp.sum(lax.all_gather(kept, axis), axis=0)]
  transfers between devices with their start and end apart: 6 -> 6, of which waited for: 6 -> 6; matrix products, arithmetic and copies ran while one was open for 2% -> 1% of each run, Pallas kernels for 0% -> 0%
where the time goes in v2:
time: 749 us; the launch traced here: 747 us
  waiting for transfers between devices  685 us (91%)
  matrix products  25.8 us (3%)
  between operations  14.2 us (2%)
  local copies, waits for them, and re-layouts  12.7 us (2%)
  other arithmetic  8.79 us (1%)
    psum x1, waiting for transfers between devices, per_device(): small = lax.psum(mult(panel.T, scaled), ('row', 'col'))  254 us
    unnamed x7, waiting for transfers between devices  216 us
    all_gather x1, waiting for transfers between devices, per_device(): row_panel = lax.all_gather(panel, 'col', axis=0, tiled=True)  82.3 us
    all_gather x1, waiting for transfers between devices, per_device(): row_corr = lax.all_gather(correction, 'col', axis=0, tiled=True)  76.5 us
    all_gather x2, waiting for transfers between devices, from_root(): return jnp.sum(lax.all_gather(kept, axis), axis=0)  56.1 us
    dot_general x7, matrix products, mult(): jnp.dot(left, right, precision=lax.Precision.HIGHEST, preferred_element_t...  25.8 us
  transfers between devices with their start and end apart: 6, of which 6 were waited for; matrix products, arithmetic and copies ran while one was open for 1% of the time, Pallas kernels for 0%

profile of v2, /device:TPU:8, one launch (start us, length us, event | category | flops | bytes accessed | tf_op | source)
XLA Modules:
  0.0 747.0 jit_solution(338329593688970784)
XLA Ops:
  7.2 0.0 copy-start
  7.2 0.0 all-gather.7.cloned.1.call-start
  7.2 0.7 all-gather.7.cloned.1.call-update
  7.9 0.0 all-gather.11.cloned.1.call-start
  8.0 82.3 %all-gather.7.cloned.1.call-done = f32[2048,256]{1,0:T(8,128)} async-done(((f32[64,256]{1,0:T(8,128)}), f32[2048,256]{1,0:T(8,128)}) %all-gather.7.cloned.1.call-update) | async-done | bytes 2097168 | tf_op jit(solution)/shard_map/all_gather | solution.py:24
  90.3 1.9 dynamic-slice_select_fusion.1
  92.1 0.0 all-gather.11.cloned.1.call-update
  92.2 0.0 reduce-scatter.4.cloned.1.call-start
  92.2 33.6 %all-gather.11.cloned.1.call-done = f32[4096,256]{1,0:T(8,128)} async-done(((f32[512,256]{1,0:T(8,128)}), f32[4096,256]{1,0:T(8,128)}) %all-gather.11.cloned.1.call-update) | async-done | bytes 4194320 | tf_op jit(solution)/shard_map/all_gather | solution.py:9
  125.8 2.5 reduce_sum.18
  128.3 8.6 %convolution_bitcast_fusion = f32[2048,256]{0,1:T(8,128)S(1)} fusion(f32[512,256]{1,0:T(8,128)S(1)} %reduce_sum.18, f32[2048,512]{1,0:T(8,128)} %param.3), kind=kOutput, calls=%fused_computation.2 | convolution fusion | flops 3221225472 | bytes 6815744 | tf_op jit(solution)/shard_map/dot_general | solution.py:13
  136.9 0.0 copy-start.3
  136.9 1.8 copy.12
  138.8 0.0 reduce-scatter.4.cloned.1.call-update
  138.8 0.0 all-reduce.2.cloned.1.call-start
  138.8 215.5 %reduce-scatter.4.cloned.1.call-done = f32[64,256]{1,0:T(8,128)} async-done(((f32[2048,256]{1,0:T(8,128)}), f32[64,256]{1,0:T(8,128)}) %reduce-scatter.4.cloned.1.call-update) | async-done | bytes 65552
  354.4 0.0 copy-done
  354.4 1.1 fusion.3
  355.5 0.0 copy-done.3
  355.5 1.1 convolution_bitcast_fusion.1
  356.6 0.0 all-reduce.2.cloned.1.call-update
  356.6 0.0 all-gather.9.cloned.1.call-start
  356.7 254.0 %all-reduce.2.cloned.1.call-done = f32[256,256]{0,1:T(8,128)} async-done(((f32[256,256]{0,1:T(8,128)}), f32[256,256]{0,1:T(8,128)}) %all-reduce.2.cloned.1.call-update) | async-done | bytes 262160 | tf_op jit(solution)/shard_map/psum | solution.py:28
  610.7 1.3 fusion.4
  612.0 1.0 fusion.2
  613.0 0.0 all-gather.9.cloned.1.call-update
  613.0 0.0 all-gather.13.cloned.1.call-start
  613.1 76.5 %all-gather.9.cloned.1.call-done = f32[2048,256]{1,0:T(8,128)} async-done(((f32[64,256]{1,0:T(8,128)}), f32[2048,256]{1,0:T(8,128)}) %all-gather.9.cloned.1.call-update) | async-done | bytes 2097168 | tf_op jit(solution)/shard_map/all_gather | solution.py:30
  689.6 1.9 dynamic-slice_select_fusion
  691.5 0.0 all-gather.13.cloned.1.call-update
  691.5 0.0 copy-start.1
  691.5 5.5 copy.8
  697.0 0.0 copy-done.1
  697.0 5.1 fusion.5
  702.1 0.0 copy-start.2
  702.1 22.6 %all-gather.13.cloned.1.call-done = f32[4096,256]{1,0:T(8,128)} async-done(((f32[512,256]{1,0:T(8,128)}), f32[4096,256]{1,0:T(8,128)}) %all-gather.13.cloned.1.call-update) | async-done | bytes 4194320 | tf_op jit(solution)/shard_map/all_gather | solution.py:9
  724.7 2.5 reduce_sum.19
  727.2 0.0 copy-done.2
  727.2 7.6 %fusion = f32[2048,512]{0,1:T(8,128)} fusion(f32[2048,512]{0,1:T(8,128)} %fusion.5, f32[2048,512]{0,1:T(8,128)} %copy.8, f32[512,256]{1,0:T(8,128)S(1)} %reduce_sum.19, f32[2048,256]{1,0:T(8,128)S(1)} %copy-done.2), kind=kOutput, calls=%fused_computation.1 | convolution fusion | flops 3223322624 | bytes 15204352 | tf_op jit(solution)/shard_map/dot_general | solution.py:13
  734.8 5.3 copy.10
Async XLA Ops:
  7.2 347.2 %copy-start = (f32[256,256]{1,0:T(8,128)S(1)}, f32[256,256]{1,0:T(8,128)}, u32[]{:S(2)}) copy-start(f32[256,256]{1,0:T(8,128)} %param.5) | copy-start | bytes 786436
  7.2 83.1 %all-gather.7.cloned.1.call-start = ((), (), s32[]{:S(2)}) async-start(), calls=%async_computation.1 | async-start | bytes 2162688 | tf_op jit(solution)/shard_map/all_gather | solution.py:24
  7.9 117.9 %all-gather.11.cloned.1.call-start = ((), (), s32[]{:S(2)}) async-start(), calls=%async_computation.4 | async-start | bytes 4718592 | tf_op jit(solution)/shard_map/all_gather | solution.py:9
  92.2 262.2 %reduce-scatter.4.cloned.1.call-start = ((), (), s32[]{:S(2)}) async-start(), calls=%async_computation.6 | async-start | bytes 2162688
  136.9 218.5 %copy-start.3 = (f32[64,256]{1,0:T(8,128)S(1)}, f32[64,256]{1,0:T(8,128)}, u32[]{:S(2)}) copy-start(f32[64,256]{1,0:T(8,128)} %param.4) | copy-start | bytes 196612
  138.8 471.9 %all-reduce.2.cloned.1.call-start = ((), (), s32[]{:S(2)}) async-start(), calls=%async_computation.2 | async-start | bytes 524288 | tf_op jit(solution)/shard_map/psum | solution.py:28
  356.6 332.9 %all-gather.9.cloned.1.call-start = ((), (), s32[]{:S(2)}) async-start(), calls=%async_computation.3 | async-start | bytes 2162688 | tf_op jit(solution)/shard_map/all_gather | solution.py:30
  613.0 111.6 %all-gather.13.cloned.1.call-start = ((), (), s32[]{:S(2)}) async-start(), calls=%async_computation.5 | async-start | bytes 4718592 | tf_op jit(solution)/shard_map/all_gather | solution.py:9
  691.5 5.5 copy-start.1
  702.1 25.1 %copy-start.2 = (f32[2048,256]{1,0:T(8,128)S(1)}, f32[2048,256]{1,0:T(8,128)}, u32[]{:S(2)}) copy-start(f32[2048,256]{1,0:T(8,128)} %all-gather.7.cloned.1.call-done) | copy-start | bytes 6291460
Sparse Core Ops, SparseCore 0:
  10.6 79.6 all-gather.6
  92.7 33.0 all-gather.10
  138.9 215.4 reduce-scatter.3
  361.2 249.4 all-reduce.1
  614.0 75.5 all-gather.8
  691.6 33.0 all-gather.12
